TPU v7x, 512 devices: a whole 4x4x16 slice. The times are simulated.
512 devices in a mesh: sim: 64 (over z, y), lens: 8 (over x, core).
Axes of the slice: x: 4, y: 4, z: 16, core: 2. Of those that a mesh axis runs over, the one named last changes fastest.
Arguments:
- patches: bfloat16 [65536, 2, 2048], P(('sim', 'lens')), may hold values from -6 to 6
- patch_cycle: int32 [65536, 1], P(('sim', 'lens')), may hold values from 0 to 63; in each aligned block of 128 rows (0 to 127, 128 to 255, ...) at most 4 rows name the same one
- patch_block: int32 [65536], P(('sim', 'lens')), may hold values from 0 to 7
- m_values: int32 [128], replicated, may hold values from 0 to 8191, as said below
- shell_weight: float32 [2], replicated, may hold values from 0.5 to 2
- legendre_panel: bfloat16 [128, 512, 8192], P('sim', 'lens'), as said below
- spin2_panel: bfloat16 [128, 512, 8192], P('sim', 'lens'), as said below
Outputs:
- kappa_modes: float32 [128, 2, 512], P('sim', None, 'lens')
- shear_modes: float32 [128, 2, 512], P('sim', None, 'lens')
Inputs may be any that keep to these rules, and one draw needn't show every extreme that they name: `patch_cycle`: among the 128 patches of one device, at most 4 lie on one cycle; some device reaches 4. `m_values`: the 128 orders are distinct; slots 2 d and 2 d + 1 hold m and 8191 - m with m below 4096, and some sim index holds 0 and 8191. legendre_panel[j, g, l] is 0 for l < 128 * (m_values[j] // 128). spin2_panel[j, g, l] is 0 for l < 128 * (m_values[j] // 128).
All inputs are finite; a program needn't handle non-finite values.
Results may differ from a plain program's by a relative error of at most 0.014.
Values may be sent and summed in bfloat16 or wider, within the bound.
A program may use at most 64 MiB of HBM per device.

v0:
```python
import math

import jax
import jax.numpy as jnp
from jax import lax
from jax.sharding import PartitionSpec as P

NPIX = 16384
BPX = 2048
LMAX = 8192
SHELLS = 2
NBLK = 8


def base_table(m_values):
    pixel = jnp.arange(BPX, dtype=jnp.int32)
    angle_index = pixel[:, None] * m_values[None, :] % NPIX
    angle = angle_index.astype(jnp.float32) * (2.0 * math.pi / NPIX)
    return jnp.concatenate([jnp.cos(angle), jnp.sin(angle)], axis=1)


def fourier_rows(rows, phase, m_values, table):
    number = rows.shape[0]
    flat = rows.reshape(number * SHELLS, BPX)
    sums = jnp.dot(flat, table, precision=lax.Precision.HIGHEST).reshape(number, SHELLS, 2, -1)
    cosine_part = sums[:, :, 0]
    sine_part = sums[:, :, 1]
    turn_index = phase[:, None] * m_values[None, :] % (2 * NPIX)
    turn = turn_index.astype(jnp.float32) * (math.pi / NPIX)
    turn_cos = jnp.cos(turn)[:, None, :]
    turn_sin = jnp.sin(turn)[:, None, :]
    real_part = turn_cos * cosine_part - turn_sin * sine_part
    imag_part = -(turn_sin * cosine_part + turn_cos * sine_part)
    return jnp.stack([real_part, imag_part], axis=2) / math.sqrt(NPIX)


def on_device(
    patches, patch_cycle, patch_block, m_values, shell_weight, legendre_panel, spin2_panel
):
    n_sim = lax.axis_size("sim")
    n_lens = lax.axis_size("lens")
    sim_rank = lax.axis_index("sim")
    lens_rank = lax.axis_index("lens")
    number = patches.shape[0]
    m_dev = legendre_panel.shape[0]
    table = base_table(m_values)
    destination = patch_cycle[:, 0]
    capacity = max(2, (2 * number + n_sim - 1) // n_sim)
    onehot_int = (destination[:, None] == jnp.arange(n_sim, dtype=jnp.int32)[None, :]).astype(
        jnp.int32
    )
    before = jnp.cumsum(onehot_int, axis=0) - onehot_int
    slot = jnp.sum(before * onehot_int, axis=1)
    outgoing = (
        jnp.zeros((n_sim, capacity, SHELLS, BPX), jnp.bfloat16).at[destination, slot].set(patches)
    )
    block_onehot = jax.nn.one_hot(patch_block, NBLK, dtype=jnp.bfloat16)
    selector = (
        jnp.zeros((n_sim, capacity, NBLK), jnp.bfloat16).at[destination, slot].set(block_onehot)
    )
    incoming, chosen = (
        lax.all_to_all(outgoing, "sim", split_axis=0, concat_axis=0, tiled=True),
        lax.all_to_all(selector, "sim", split_axis=0, concat_axis=0, tiled=True),
    )
    cycle = jnp.einsum("qcb,qcsp->bsp", chosen, incoming, preferred_element_type=jnp.float32)
    parity = (lens_rank * n_sim + sim_rank) % 2
    phase = 2 * jnp.arange(NBLK, dtype=jnp.int32) * BPX + parity
    modes = jnp.sum(fourier_rows(cycle, phase, m_values, table), axis=0)
    packed = modes.astype(jnp.bfloat16).reshape(SHELLS * 2, n_sim, m_dev).transpose(1, 0, 2)
    local_modes = lax.all_to_all(packed, "sim", split_axis=0, concat_axis=0, tiled=True)
    delta = jnp.einsum(
        "rxj,jrl->jxl", local_modes, legendre_panel, preferred_element_type=jnp.float32
    )
    delta = delta.reshape(m_dev, SHELLS, 2, LMAX)
    partial_kappa = jnp.zeros((m_dev, 2, LMAX), jnp.float32)
    for shell in range(SHELLS):
        partial_kappa = partial_kappa + shell_weight[shell] * delta[:, shell]
    partial_kappa = partial_kappa / math.sqrt(n_sim * n_lens)
    kappa = lax.psum(partial_kappa.astype(jnp.bfloat16), "lens").astype(jnp.float32)
    ell = jnp.arange(LMAX, dtype=jnp.int32).astype(jnp.float32)
    factor = jnp.where(
        ell >= 2.0, jnp.sqrt((ell + 2.0) * (ell - 1.0) / jnp.maximum(ell * (ell + 1.0), 1.0)), 0.0
    )
    shear = kappa * factor
    kappa_rounded = kappa.astype(jnp.bfloat16)
    shear_rounded = shear.astype(jnp.bfloat16)
    kappa_modes = jnp.einsum(
        "jcl,jrl->jcr", kappa_rounded, legendre_panel, preferred_element_type=jnp.float32
    )
    shear_modes = jnp.einsum(
        "jcl,jrl->jcr", shear_rounded, spin2_panel, preferred_element_type=jnp.float32
    )
    scale = 1.0 / math.sqrt(LMAX)
    return (kappa_modes * scale, shear_modes * scale)


def solution(mesh):
    placed = (
        P(("sim", "lens"), None, None),
        P(("sim", "lens"), None),
        P(("sim", "lens")),
        P(),
        P(),
        P("sim", "lens", None),
        P("sim", "lens", None),
    )
    return jax.shard_map(
        on_device,
        mesh=mesh,
        in_specs=placed,
        out_specs=(P("sim", None, "lens"), P("sim", None, "lens")),
        check_vma=False,
    )
```

profile of v0, /device:TPU:1, one launch (start us, length us, event | category | flops | bytes accessed | tf_op | source)
XLA Modules:
  0.0 287.1 jit_solution(16484851570701689378)
XLA Ops:
  7.2 0.0 copy-start
  7.2 0.0 copy-start.2
  7.2 0.9 fusion.16
  8.1 0.2 reduce_window_sum.11
  8.3 0.8 select_reduce_fusion
  9.1 0.7 fusion.33
  9.8 0.7 fusion.17
  10.5 0.6 broadcast_in_dim.9
  11.2 13.3 %scatter_fusion = bf16[64,4,8]{2,1,0:T(4,128)(2,1)} fusion(bf16[64,4,8]{2,1,0:T(4,128)(2,1)} %broadcast_in_dim.9, s32[128]{0:T(128)S(1)} %fusion.33, bf16[128,8]{1,0:T(8,128)(2,1)S(1)} %fusion.17), kind=kCustom, calls=%fused_computation | custom fusion | bytes 7168 | tf_op jit(solution)/shard_map/scatter | solution.py:59
  24.5 19.2 %all-to-all-start = ((bf16[64,4,8]{2,1,0:T(4,128)(2,1)}), bf16[64,4,8]{2,1,0:T(4,128)(2,1)S(1)}, u32[]{:S(2)}, u32[]{:S(2)}) async-start(bf16[64,4,8]{2,1,0:T(4,128)(2,1)} %scatter_fusion), calls=%async_computation | async-start | bytes 131072 | tf_op jit(solution)/shard_map/all_to_all | solution.py:63
  43.7 3.3 %broadcast_in_dim.10 = bf16[64,4,2,2048]{3,2,1,0:T(2,128)(2,1)} broadcast(bf16[]{:T(256)} %constant.76.clone.1), dimensions={} | broadcast | bytes 2097154 | tf_op jit(solution)/shard_map/broadcast_in_dim | solution.py:55
  47.0 0.0 copy-done.2
  47.0 16.8 %scatter_fusion.1 = bf16[64,4,2,2048]{3,2,1,0:T(2,128)(2,1)} fusion(bf16[64,4,2,2048]{3,2,1,0:T(2,128)(2,1)} %broadcast_in_dim.10, s32[128]{0:T(128)S(1)} %fusion.33, bf16[128,2,2048]{2,1,0:T(2,128)(2,1)S(1)} %copy-done.2), kind=kCustom, calls=%fused_computation.1 | custom fusion | bytes 3146752 | tf_op jit(solution)/shard_map/scatter | solution.py:55
  63.8 4.0 %copy.25 = bf16[64,4,2,2048]{3,1,2,0:T(4,128)(2,1)} copy(bf16[64,4,2,2048]{3,2,1,0:T(2,128)(2,1)} %scatter_fusion.1) | data formatting | bytes 4194304 | tf_op jit(solution)/shard_map/scatter | solution.py:55
  67.8 0.0 copy-start.3
  67.8 0.0 all-to-all-done
  67.8 15.1 %all-to-all-start.1 = ((bf16[64,4,2,2048]{3,1,2,0:T(4,128)(2,1)}), bf16[64,4,2,2048]{3,1,2,0:T(4,128)(2,1)}, u32[]{:S(2)}, u32[]{:S(2)}) async-start(bf16[64,4,2,2048]{3,1,2,0:T(4,128)(2,1)} %copy.25), calls=%async_computation.1 | async-start | bytes 4194304 | tf_op jit(solution)/shard_map/all_to_all | solution.py:62
  83.0 0.0 copy-done.3
  83.0 0.1 fusion.31
  83.1 4.1 %fusion.9 = (f32[2048,128]{0,1:T(8,128)S(1)}, f32[2048,128]{0,1:T(8,128)S(1)}) fusion(s32[128]{0:T(128)S(1)} %copy-done.3), kind=kLoop, calls=%fused_computation.17 | loop fusion | flops 3670016 | bytes 2097664 | tf_op jit(solution)/shard_map/cos | solution.py:19
  87.3 1.5 pad_maximum_fusion
  88.7 0.1 copy.26
  88.8 0.0 copy-start.4
  88.8 89.0 %all-to-all-done.1 = bf16[64,4,2,2048]{3,1,2,0:T(4,128)(2,1)} async-done(((bf16[64,4,2,2048]{3,1,2,0:T(4,128)(2,1)}), bf16[64,4,2,2048]{3,1,2,0:T(4,128)(2,1)}, u32[]{:S(2)}, u32[]{:S(2)}) %all-to-all-start.1) | async-done | bytes 2097184 | tf_op jit(solution)/shard_map/all_to_all | solution.py:62
  177.9 0.0 copy-start.1
  177.9 4.0 %fusion = f32[8,2,2048,1]{2,0,3,1:T(8,128)S(1)} fusion(bf16[64,4,2,2048]{3,1,2,0:T(4,128)(2,1)} %all-to-all-done.1, bf16[64,4,8]{0,2,1:T(8,128)(2,1)S(1)} %copy.26), kind=kOutput, calls=%fused_computation.3 | convolution fusion | flops 16777216 | bytes 2232320 | tf_op jit(solution)/shard_map/qcb,qcsp->bsp/dot_general | solution.py:65
  181.9 0.0 copy-done.1
  181.9 1.7 fusion.35
  183.7 0.2 convert_element_type.52
  183.8 1.1 copy.28
  184.9 10.0 %all-to-all-start.2 = ((bf16[64,4,2]{1,2,0:T(2,128)(2,1)}), bf16[64,4,2]{1,2,0:T(2,128)(2,1)S(1)}, u32[]{:S(2)}, u32[]{:S(2)}) async-start(bf16[64,4,2]{1,2,0:T(2,128)(2,1)} %copy.28), calls=%async_computation.2 | async-start | bytes 65536 | tf_op jit(solution)/shard_map/all_to_all | solution.py:70
  194.9 0.0 all-reduce.2.cloned.1.call-start
  195.0 0.0 copy-done.4
  195.0 0.6 fusion.34
  195.6 13.1 %all-to-all-done.2 = bf16[64,4,2]{1,2,0:T(2,128)(2,1)S(1)} async-done(((bf16[64,4,2]{1,2,0:T(2,128)(2,1)}), bf16[64,4,2]{1,2,0:T(2,128)(2,1)S(1)}, u32[]{:S(2)}, u32[]{:S(2)}) %all-to-all-start.2) | async-done | bytes 1056 | tf_op jit(solution)/shard_map/all_to_all | solution.py:70
  208.6 0.0 copy-done
  208.6 0.4 fusion.23
  209.1 0.2 reshape.114
  209.3 2.0 fusion.18
  211.3 0.0 all-reduce.2.cloned.1.call-update
  211.3 65.4 %all-reduce.2.cloned.1.call-done = bf16[2,2,8192]{2,1,0:T(2,128)(2,1)} async-done(((bf16[2,2,8192]{2,1,0:T(2,128)(2,1)}), bf16[2,2,8192]{2,1,0:T(2,128)(2,1)}) %all-reduce.2.cloned.1.call-update) | async-done | bytes 65552 | tf_op jit(solution)/shard_map/psum | solution.py:79
  276.7 0.0 copy-start.5
  276.7 0.0 copy-start.6
  276.7 2.2 convolution_multiply_fusion.1
  279.0 0.0 copy-done.5
  279.0 0.0 copy-done.6
  279.0 1.2 convolution_multiply_fusion
  (4 shorter events, 0.1 us)
Async XLA Ops:
  7.2 201.4 %copy-start = (bf16[2,64,8192]{2,1,0:T(8,128)(2,1)S(1)}, bf16[2,64,8192]{2,1,0:T(8,128)(2,1)}, u32[]{:S(2)}) copy-start(bf16[2,64,8192]{2,1,0:T(8,128)(2,1)} %param.12) | copy-start | bytes 6291460
  7.2 39.8 %copy-start.2 = (bf16[128,2,2048]{2,1,0:T(2,128)(2,1)S(1)}, bf16[128,2,2048]{2,1,0:T(2,128)(2,1)}, u32[]{:S(2)}) copy-start(bf16[128,2,2048]{2,1,0:T(2,128)(2,1)} %param.7) | copy-start | bytes 3145732
  24.5 43.4 %all-to-all-start = ((bf16[64,4,8]{2,1,0:T(4,128)(2,1)}), bf16[64,4,8]{2,1,0:T(4,128)(2,1)S(1)}, u32[]{:S(2)}, u32[]{:S(2)}) async-start(bf16[64,4,8]{2,1,0:T(4,128)(2,1)} %scatter_fusion), calls=%async_computation | async-start | bytes 131072 | tf_op jit(solution)/shard_map/all_to_all | solution.py:63
  67.8 15.1 %copy-start.3 = (s32[128]{0:T(128)S(1)}, s32[128]{0:T(128)}, u32[]{:S(2)}) copy-start(s32[128]{0:T(128)} %param.10) | copy-start | bytes 1540
  67.8 110.0 %all-to-all-start.1 = ((bf16[64,4,2,2048]{3,1,2,0:T(4,128)(2,1)}), bf16[64,4,2,2048]{3,1,2,0:T(4,128)(2,1)}, u32[]{:S(2)}, u32[]{:S(2)}) async-start(bf16[64,4,2,2048]{3,1,2,0:T(4,128)(2,1)} %copy.25), calls=%async_computation.1 | async-start | bytes 4194304 | tf_op jit(solution)/shard_map/all_to_all | solution.py:62
  88.8 106.1 %copy-start.4 = (f32[2]{0:T(128)S(1)}, f32[2]{0:T(128)}, u32[]{:S(2)}) copy-start(f32[2]{0:T(128)} %param.11) | copy-start | bytes 28
  177.9 4.0 %copy-start.1 = (f32[2048,256]{0,1:T(8,128)S(1)}, f32[2048,256]{0,1:T(8,128)}, u32[]{:S(2)}) copy-start(f32[2048,256]{0,1:T(8,128)} %pad_maximum_fusion) | copy-start | bytes 6291460
  184.9 23.7 %all-to-all-start.2 = ((bf16[64,4,2]{1,2,0:T(2,128)(2,1)}), bf16[64,4,2]{1,2,0:T(2,128)(2,1)S(1)}, u32[]{:S(2)}, u32[]{:S(2)}) async-start(bf16[64,4,2]{1,2,0:T(2,128)(2,1)} %copy.28), calls=%async_computation.2 | async-start | bytes 65536 | tf_op jit(solution)/shard_map/all_to_all | solution.py:70
  194.9 81.8 %all-reduce.2.cloned.1.call-start = ((), (), s32[]{:S(2)}) async-start(), calls=%async_computation.3 | async-start | bytes 131072 | tf_op jit(solution)/shard_map/psum | solution.py:79
  276.7 2.2 copy-start.5
  276.7 2.2 copy-start.6
Sparse Core Ops, SparseCore 0:
  211.4 65.2 all-reduce.1
where the time goes:
time: 288 us; the launch traced here: 287 us
  waiting for transfers between devices  167 us (58%)
  starting transfers between devices  44.3 us (15%)
  local copies, waits for them, and re-layouts  40.3 us (14%)
  between operations  14.2 us (5%)
  other arithmetic  11.1 us (4%)
  matrix products  9.65 us (3%)
    all_to_all x1, waiting for transfers between devices, on_device(): lax.all_to_all(outgoing, 'sim', split_axis=0, concat_axis=0, tiled=True)  89 us
    psum x1, waiting for transfers between devices, on_device(): lax.psum(partial_kappa.astype(jnp.bfloat16), 'lens').astype(jnp.float32)  65.4 us
    scatter x2, local copies, waits for them, and re-layouts, on_device(): jnp.zeros((n_sim, capacity, SHELLS, BPX), jnp.bfloat16)  20.8 us
    all_to_all x1, starting transfers between devices, on_device(): lax.all_to_all(selector, 'sim', split_axis=0, concat_axis=0, tiled=True)  19.2 us
    all_to_all x1, starting transfers between devices, on_device(): lax.all_to_all(outgoing, 'sim', split_axis=0, concat_axis=0, tiled=True)  15.1 us
    scatter x1, local copies, waits for them, and re-layouts, on_device(): jnp.zeros((n_sim, capacity, NBLK), jnp.bfloat16).at[destination, slot]  13.3 us
    all_to_all x1, waiting for transfers between devices, on_device(): lax.all_to_all(packed, 'sim', split_axis=0, concat_axis=0, tiled=True)  13.1 us
    all_to_all x1, starting transfers between devices, on_device(): lax.all_to_all(packed, 'sim', split_axis=0, concat_axis=0, tiled=True)  9.96 us
  transfers between devices with their start and end apart: 4, of which 3 were waited for; matrix products, arithmetic and copies ran while one was open for 11% of the time, Pallas kernels for 0%

commit v1 on v0

v1 whole, which is shorter than its diff:
```python
import math

import jax
import jax.numpy as jnp
from jax import lax
from jax.experimental import pallas as pl
from jax.experimental.pallas import tpu as pltpu
from jax.sharding import PartitionSpec as P

NPIX = 16384
BPX = 2048
LMAX = 8192
SHELLS = 2
NZ = 16
NY = 4
NLENS = 8
K_DEV = 128
ROWS = K_DEV * SHELLS
LCHUNK = LMAX // NLENS
MESH = pl.DeviceIdType.MESH
F32 = jnp.float32
BF16 = jnp.bfloat16


def split(value):
    high = value.astype(BF16)
    return high, (value - high.astype(F32)).astype(BF16)


def mxu(a, b):
    return jnp.dot(a, b, preferred_element_type=F32)


def cos_sin(index):
    quarter = (index + 4096) >> 13
    t = (index - (quarter << 13)).astype(F32) * (2.0 * math.pi / 32768)
    t2 = t * t
    c = 1.0 + t2 * (-0.5 + t2 * (1 / 24 + t2 * (-1 / 720 + t2 * (1 / 40320))))
    s = t * (1.0 + t2 * (-1 / 6 + t2 * (1 / 120 + t2 * (-1 / 5040 + t2 * (1 / 362880)))))
    odd = (quarter & 1) == 1
    cosine = jnp.where(odd, s, c)
    sine = jnp.where(odd, c, s)
    cosine = jnp.where(((quarter + 1) & 2) == 2, -cosine, cosine)
    sine = jnp.where((quarter & 2) == 2, -sine, sine)
    return cosine, sine


def iota(shape, dim):
    return lax.broadcasted_iota(jnp.int32, shape, dim)


def kernel(
    cycle_hbm, block_hbm, m_hbm, weight, x_hbm, l_hbm, s_hbm,
    kappa_out, shear_out,
    small, xv, lv, sv, table_hi, table_lo, base, turn, factor,
    part, recv_y, summed, recv_z, kpart, recv_k, kfull,
    small_sem, x_sem, panel_sem,
    send_y, got_y, send_z, got_z, send_k, got_k, send_g, got_g,
):
    sim = lax.axis_index("sim")
    lens = lax.axis_index("lens")
    z = sim // NY
    y = sim % NY

    def sim_id(z_to, y_to):
        return (z_to * NY + y_to, lens)

    barrier = pltpu.get_barrier_semaphore()
    for d in range(1, NZ):
        pl.semaphore_signal(
            barrier, inc=1, device_id=sim_id((z + d) % NZ, y), device_id_type=MESH
        )
    for d in range(1, NY):
        pl.semaphore_signal(
            barrier, inc=1, device_id=sim_id(z, (y + d) % NY), device_id_type=MESH
        )
    for d in range(1, NLENS):
        pl.semaphore_signal(
            barrier, inc=1, device_id=(sim, (lens + d) % NLENS), device_id_type=MESH
        )

    small_copies = [
        pltpu.make_async_copy(source, small.at[i], small_sem.at[i])
        for i, source in enumerate((cycle_hbm, block_hbm, m_hbm))
    ]
    for copy in small_copies:
        copy.start()
    x_copies = [
        pltpu.make_async_copy(
            x_hbm.at[:, :, pl.ds(512 * i, 512)], xv.at[:, :, pl.ds(512 * i, 512)], x_sem.at[i]
        )
        for i in range(4)
    ]
    for copy in x_copies:
        copy.start()
    l_copy = pltpu.make_async_copy(l_hbm, lv, panel_sem.at[0])
    s_copy = pltpu.make_async_copy(s_hbm, sv, panel_sem.at[1])
    l_copy.start()
    s_copy.start()
    for copy in small_copies:
        copy.wait()

    cycle_row = small[0]
    block_row = small[1]
    m_row = jnp.broadcast_to(small[2], (8, 128))
    row = iota((128, 128), 0)
    column = iota((128, 128), 1)
    slot = 8 * (column & 15) + 2 * ((column >> 4) & 3) + (column >> 6)
    permute = (row == slot).astype(BF16)
    m_high = mxu((m_row >> 6).astype(F32).astype(BF16), permute)
    m_low = mxu((m_row & 63).astype(F32).astype(BF16), permute)
    orders = (m_high * 64.0 + m_low).astype(jnp.int32)[0:1]

    a_cos, a_sin = cos_sin((128 * iota((32, 128), 0) * orders) & 32767)
    base[0, 0:32] = a_cos
    base[1, 0:32] = a_sin
    b_cos, b_sin = cos_sin((2 * iota((64, 128), 0) * orders) & 32767)

    def fill(a, carry):
        ca = base[0, pl.ds(a, 1), :]
        sa = base[1, pl.ds(a, 1), :]
        rows = pl.ds(pl.multiple_of(a * 64, 64), 64)
        c_high, c_low = split(ca * b_cos - sa * b_sin)
        s_high, s_low = split(sa * b_cos + ca * b_sin)
        table_hi[rows, 0:128] = c_high
        table_hi[rows, 128:256] = s_high
        table_lo[rows, 0:128] = c_low
        table_lo[rows, 128:256] = s_low
        return carry

    lax.fori_loop(0, 32, fill, 0)

    code = (block_row * 64 + cycle_row).astype(F32)
    row2 = iota((ROWS, 128), 0)
    picked = jnp.where(iota((ROWS, 128), 1) == (row2 >> 1), code, 0.0)
    code_column = jnp.sum(picked, axis=1, keepdims=True).astype(jnp.int32)
    phase = (code_column >> 6) * (2 * BPX) + (code_column & 1)
    turn_cos, turn_sin = cos_sin((phase * orders) & 32767)
    scale = 1.0 / (math.sqrt(NPIX) * math.sqrt(NZ * NY * NLENS))
    row_weight = jnp.where((row2 & 1) == 0, weight[0], weight[1]) * scale
    turn[0] = turn_cos * row_weight
    turn[1] = turn_sin * row_weight
    spread = (iota((128, ROWS), 0) == (iota((128, ROWS), 1) >> 1)).astype(BF16)
    cycle_wide = mxu(
        jnp.broadcast_to(cycle_row, (8, 128)).astype(F32).astype(BF16), spread
    )[0:1]
    onehot = ((iota((128, ROWS), 0) & 63).astype(F32) == cycle_wide).astype(F32).astype(BF16)

    ell = (LCHUNK * iota((8, LCHUNK), 0) + iota((8, LCHUNK), 1)).astype(F32)
    factor[...] = jnp.where(
        ell >= 2.0,
        jnp.sqrt((ell + 2.0) * (ell - 1.0) / jnp.maximum(ell * (ell + 1.0), 1.0)),
        0.0,
    )

    total = jnp.zeros((ROWS, 256), F32)
    for i in range(8):
        if i % 2 == 0:
            x_copies[i // 2].wait()
        piece = xv[:, :, 256 * i : 256 * i + 256].reshape(ROWS, 256)
        total = total + mxu(piece, table_hi[256 * i : 256 * i + 256])
        total = total + mxu(piece, table_lo[256 * i : 256 * i + 256])
    zc = total[:, 0:128]
    zs = total[:, 128:256]
    real = turn[0] * zc - turn[1] * zs
    imag = -(turn[1] * zc + turn[0] * zs)
    high, low = split(jnp.concatenate([real, imag], axis=1))
    gathered = mxu(onehot, high) + mxu(onehot, low)
    left = iota((64, 128), 1) < 64
    for c in range(2):
        turned = gathered[:, 128 * c : 128 * c + 128].T
        part[:, c, :] = jnp.where(left, turned[0:64], turned[64:128])

    pl.semaphore_wait(barrier, NZ - 1 + NY - 1 + NLENS - 1)

    copies = []
    for d in range(1, NY):
        y_to = (y + d) % NY
        copy = pltpu.make_async_remote_copy(
            src_ref=part.at[pl.ds(y_to * NZ, NZ)],
            dst_ref=recv_y.at[d - 1],
            send_sem=send_y.at[d - 1],
            recv_sem=got_y.at[d - 1],
            device_id=sim_id(z, y_to),
            device_id_type=MESH,
        )
        copy.start()
        copies.append(copy)
    for copy in copies:
        copy.wait_recv()
    summed[...] = part[pl.ds(y * NZ, NZ)] + recv_y[0] + (recv_y[1] + recv_y[2])
    for d in range(1, NZ):
        z_to = (z + d) % NZ
        copy = pltpu.make_async_remote_copy(
            src_ref=summed.at[z_to],
            dst_ref=recv_z.at[d - 1],
            send_sem=send_z.at[d - 1],
            recv_sem=got_z.at[d - 1],
            device_id=sim_id(z_to, y),
            device_id_type=MESH,
        )
        copy.start()
        copies.append(copy)
    l_copy.wait()
    s_copy.wait()
    for copy in copies[NY - 1 :]:
        copy.wait_recv()
    modes = summed[z]
    for d in range(NZ - 1):
        modes = modes + recv_z[d]

    side = iota((2, 128), 1) < 64
    rows4 = jnp.concatenate(
        [
            jnp.where(side, modes, 0.0),
            jnp.where(side, 0.0, modes),
            jnp.zeros((4, 128), F32),
        ],
        axis=0,
    ).astype(BF16)
    for i in range(NLENS):
        columns = slice(LCHUNK * i, LCHUNK * (i + 1))
        kappa = mxu(rows4, lv[:, :, columns].reshape(128, LCHUNK))
        kpart[i] = kappa[0:4].astype(BF16)

    copies_k = []
    for d in range(1, NLENS):
        lens_to = (lens + d) % NLENS
        copy = pltpu.make_async_remote_copy(
            src_ref=kpart.at[lens_to],
            dst_ref=recv_k.at[d - 1],
            send_sem=send_k.at[d - 1],
            recv_sem=got_k.at[d - 1],
            device_id=(sim, lens_to),
            device_id_type=MESH,
        )
        copy.start()
        copies_k.append(copy)
    for copy in copies_k:
        copy.wait_recv()
    kappa = kpart[lens].astype(F32)
    for d in range(NLENS - 1):
        kappa = kappa + recv_k[d].astype(F32)
    kfull[lens] = kappa.astype(BF16)
    copies_g = []
    for d in range(1, NLENS):
        lens_to = (lens + d) % NLENS
        copy = pltpu.make_async_remote_copy(
            src_ref=kfull.at[lens],
            dst_ref=kfull.at[lens],
            send_sem=send_g.at[d - 1],
            recv_sem=got_g.at[d - 1],
            device_id=(sim, lens_to),
            device_id_type=MESH,
        )
        copy.start()
        copies_g.append(copy)
    for copy in copies_g:
        copy.wait_recv()

    pad = jnp.zeros((4, LCHUNK), F32)
    out_k = jnp.zeros((8, 128), F32)
    out_s = jnp.zeros((8, 128), F32)
    contract = (((1,), (1,)), ((), ()))
    for i in range(NLENS):
        columns = slice(LCHUNK * i, LCHUNK * (i + 1))
        kappa = jnp.concatenate([kfull[i].astype(F32), pad], axis=0)
        shear = kappa * factor[i : i + 1, :]
        out_k = out_k + lax.dot_general(
            kappa.astype(BF16),
            lv[:, :, columns].reshape(128, LCHUNK),
            contract,
            preferred_element_type=F32,
        )
        out_s = out_s + lax.dot_general(
            shear.astype(BF16),
            sv[:, :, columns].reshape(128, LCHUNK),
            contract,
            preferred_element_type=F32,
        )
    scale = 1.0 / math.sqrt(LMAX)
    for b in range(2):
        kappa_out[b] = out_k[2 * b : 2 * b + 2, 64 * b : 64 * b + 64] * scale
        shear_out[b] = out_s[2 * b : 2 * b + 2, 64 * b : 64 * b + 64] * scale
    for copy in copies + copies_k + copies_g:
        copy.wait_send()


def on_device(
    patches, patch_cycle, patch_block, m_values, shell_weight, legendre_panel, spin2_panel
):
    hbm = pl.BlockSpec(memory_space=pl.ANY)
    vmem = pl.BlockSpec(memory_space=pltpu.VMEM)
    shape = jax.ShapeDtypeStruct((2, 2, 64), F32)
    dma = pltpu.SemaphoreType.DMA
    return pl.pallas_call(
        kernel,
        out_shape=(shape, shape),
        in_specs=[hbm, hbm, hbm, pl.BlockSpec(memory_space=pltpu.SMEM), hbm, hbm, hbm],
        out_specs=(vmem, vmem),
        scratch_shapes=[
            pltpu.VMEM((3, 1, 128), jnp.int32),
            pltpu.VMEM((K_DEV, SHELLS, BPX), BF16),
            pltpu.VMEM((2, 64, LMAX), BF16),
            pltpu.VMEM((2, 64, LMAX), BF16),
            pltpu.VMEM((BPX, 256), BF16),
            pltpu.VMEM((BPX, 256), BF16),
            pltpu.VMEM((2, 32, 128), F32),
            pltpu.VMEM((2, ROWS, 128), F32),
            pltpu.VMEM((8, LCHUNK), F32),
            pltpu.VMEM((NY * NZ, 2, 128), F32),
            pltpu.VMEM((NY - 1, NZ, 2, 128), F32),
            pltpu.VMEM((NZ, 2, 128), F32),
            pltpu.VMEM((NZ - 1, 2, 128), F32),
            pltpu.VMEM((NLENS, 4, LCHUNK), BF16),
            pltpu.VMEM((NLENS - 1, 4, LCHUNK), BF16),
            pltpu.VMEM((NLENS, 4, LCHUNK), BF16),
            dma((3,)),
            dma((4,)),
            dma((2,)),
            dma((NY - 1,)),
            dma((NY - 1,)),
            dma((NZ - 1,)),
            dma((NZ - 1,)),
            dma((NLENS - 1,)),
            dma((NLENS - 1,)),
            dma((NLENS - 1,)),
            dma((NLENS - 1,)),
        ],
        compiler_params=pltpu.CompilerParams(collective_id=0, has_side_effects=True),
        name="shear_step",
    )(
        patch_cycle.reshape(1, K_DEV),
        patch_block.reshape(1, K_DEV),
        m_values.reshape(1, 128),
        shell_weight,
        patches,
        legendre_panel,
        spin2_panel,
    )


def solution(mesh):
    placed = (
        P(("sim", "lens"), None, None),
        P(("sim", "lens"), None),
        P(("sim", "lens")),
        P(),
        P(),
        P("sim", "lens", None),
        P("sim", "lens", None),
    )
    return jax.shard_map(
        on_device,
        mesh=mesh,
        in_specs=placed,
        out_specs=(P("sim", None, "lens"), P("sim", None, "lens")),
        check_vma=False,
    )
```

time: 288 us -> 42.3 us (0.15)
  waiting for transfers between devices: 167 us -> 0 us
  starting transfers between devices: 44.3 us -> 0 us
  Pallas kernels: 0 us -> 39 us
  local copies, waits for them, and re-layouts: 40.3 us -> 2.48 us
  between operations: 14.2 us -> 0.64 us
  other arithmetic: 11.1 us -> 0 us
  matrix products: 9.65 us -> 0 us
    all_to_all x3 -> x0, waiting for transfers between devices: 102 us -> none  [the longest x1 89 us: on_device(): lax.all_to_all(outgoing, 'sim', split_axis=0, concat_axis=0, tiled=True)]
    psum x1 -> x0, waiting for transfers between devices: 65.4 us -> none  [on_device(): lax.psum(partial_kappa.astype(jnp.bfloat16), 'lens').astype(jnp.float32)]
    all_to_all x3 -> x0, starting transfers between devices: 44.3 us -> none  [the longest x1 19.2 us: on_device(): lax.all_to_all(selector, 'sim', split_axis=0, concat_axis=0, tiled=True)]
    pallas_call x0 -> x1, Pallas kernels: none -> 39 us  [on_device(): pl.pallas_call(kernel, out_shape=(shape, shape), in_specs=[hbm, hbm, hbm,...]
    scatter x3 -> x0, local copies, waits for them, and re-layouts: 34.1 us -> none  [the longest x2 20.8 us: on_device(): jnp.zeros((n_sim, capacity, SHELLS, BPX), jnp.bfloat16)]
    dot_general x5 -> x0, matrix products: 9.65 us -> none  [the longest x1 4.02 us: on_device(): jnp.einsum('qcb,qcsp->bsp', chosen, incoming, preferred_element_type=jnp....]
    cos x2 -> x0, other arithmetic: 4.25 us -> none  [the longest x1 4.13 us: base_table(): return jnp.concatenate([jnp.cos(angle), jnp.sin(angle)], axis=1)]
    broadcast_in_dim x2 -> x0, local copies, waits for them, and re-layouts: 3.97 us -> none  [the longest x1 3.33 us: on_device(): jnp.zeros((n_sim, capacity, SHELLS, BPX), jnp.bfloat16)]
  transfers between devices with their start and end apart: 4 -> 0, of which waited for: 3 -> 0; matrix products, arithmetic and copies ran while one was open for 11% -> 0% of each run, Pallas kernels for 0% -> 0%
where the time goes in v1:
time: 42.3 us; the launch traced here: 42.1 us
  Pallas kernels  39 us (92%)
  local copies, waits for them, and re-layouts  2.48 us (6%)
  between operations  0.64 us (2%)
    pallas_call x1, Pallas kernels, on_device(): pl.pallas_call(kernel, out_shape=(shape, shape), in_specs=[hbm, hbm, hbm,...  39 us
    unnamed x2, local copies, waits for them, and re-layouts  2.48 us

profile of v1, /device:TPU:1, one launch (start us, length us, event | category | flops | bytes accessed | tf_op | source)
XLA Modules:
  0.0 42.1 jit_solution(8354477739327839750)
XLA Ops:
  0.6 39.0 %shear_step.1 = (f32[2,2,64]{2,1,0:T(2,128)}, f32[2,2,64]{2,1,0:T(2,128)}) custom-call(s32[1,128]{1,0:T(1,128)} %bitcast.3, s32[1,128]{1,0:T(1,128)} %bitcast.4, s32[1,128]{1,0:T(1,128)} %bitcast.5, f32[2]{0:T(128)} %weight.1, bf16[128,2,2048]{2,1,0:T(2,128)(2,1)} %x_hbm.1, bf16[2,64,8192]{2,1,0:T(8,128)(2,1)} %l_hbm.1, bf16[2,64,8192]{2,1,0:T(8,128)(2,1)} %s_hbm.1), custom_call_target="tpu_custom_call" | custom-call | tf_op jit(solution)/shard_map/shear_step/pallas_call | solution.py:296
  39.6 1.2 %copy.11 = f32[2,2,64]{2,1,0:T(2,128)} copy(f32[2,2,64]{2,1,0:T(2,128)} %get-tuple-element.4) | data formatting | bytes 2048
  40.9 1.2 %copy.12 = f32[2,2,64]{2,1,0:T(2,128)} copy(f32[2,2,64]{2,1,0:T(2,128)} %get-tuple-element.5) | data formatting | bytes 2048

commit v2 on v1

--- a/solution.py
+++ b/solution.py
@@ -16,7 +16,11 @@
 NLENS = 8
 K_DEV = 128
 ROWS = K_DEV * SHELLS
-LCHUNK = LMAX // NLENS
+BLOCK = 128
+HALF = 33
+WIDE = HALF * BLOCK
+CHUNKS = ((0, 12), (12, 24), (24, 33))
+NEAR = 4
 MESH = pl.DeviceIdType.MESH
 F32 = jnp.float32
 BF16 = jnp.bfloat16
@@ -51,11 +55,11 @@
 
 def kernel(
     cycle_hbm, block_hbm, m_hbm, weight, x_hbm, l_hbm, s_hbm,
-    kappa_out, shear_out,
-    small, xv, lv, sv, table_hi, table_lo, base, turn, factor,
-    part, recv_y, summed, recv_z, kpart, recv_k, kfull,
-    small_sem, x_sem, panel_sem,
-    send_y, got_y, send_z, got_z, send_k, got_k, send_g, got_g,
+    raw,
+    small, xv, lv, sv, lc, sc, table_hi, table_lo, base, turn, factor,
+    part, recv_y, summed, recv_z, kpart, recv_k,
+    small_sem, x_sem, panel_sem, far,
+    send_y, got_y, send_z, got_z, send_k, got_k,
 ):
     sim = lax.axis_index("sim")
     lens = lax.axis_index("lens")
@@ -66,7 +70,8 @@
         return (z_to * NY + y_to, lens)
 
     barrier = pltpu.get_barrier_semaphore()
-    for d in range(1, NZ):
+    near = [d for d in range(1, NZ) if min(d, NZ - d) <= NEAR]
+    for d in near:
         pl.semaphore_signal(
             barrier, inc=1, device_id=sim_id((z + d) % NZ, y), device_id_type=MESH
         )
@@ -95,8 +100,6 @@
         copy.start()
     l_copy = pltpu.make_async_copy(l_hbm, lv, panel_sem.at[0])
     s_copy = pltpu.make_async_copy(s_hbm, sv, panel_sem.at[1])
-    l_copy.start()
-    s_copy.start()
     for copy in small_copies:
         copy.wait()
 
@@ -146,13 +149,6 @@
     )[0:1]
     onehot = ((iota((128, ROWS), 0) & 63).astype(F32) == cycle_wide).astype(F32).astype(BF16)
 
-    ell = (LCHUNK * iota((8, LCHUNK), 0) + iota((8, LCHUNK), 1)).astype(F32)
-    factor[...] = jnp.where(
-        ell >= 2.0,
-        jnp.sqrt((ell + 2.0) * (ell - 1.0) / jnp.maximum(ell * (ell + 1.0), 1.0)),
-        0.0,
-    )
-
     total = jnp.zeros((ROWS, 256), F32)
     for i in range(8):
         if i % 2 == 0:
@@ -160,6 +156,8 @@
         piece = xv[:, :, 256 * i : 256 * i + 256].reshape(ROWS, 256)
         total = total + mxu(piece, table_hi[256 * i : 256 * i + 256])
         total = total + mxu(piece, table_lo[256 * i : 256 * i + 256])
+    l_copy.start()
+    s_copy.start()
     zc = total[:, 0:128]
     zs = total[:, 128:256]
     real = turn[0] * zc - turn[1] * zs
@@ -171,7 +169,9 @@
         turned = gathered[:, 128 * c : 128 * c + 128].T
         part[:, c, :] = jnp.where(left, turned[0:64], turned[64:128])
 
-    pl.semaphore_wait(barrier, NZ - 1 + NY - 1 + NLENS - 1)
+    pl.semaphore_wait(barrier, len(near) + NY - 1 + NLENS - 1)
+    for d in (NEAR, NZ - NEAR):
+        pl.semaphore_signal(far, inc=1, device_id=sim_id((z + d) % NZ, y), device_id_type=MESH)
 
     copies = []
     for d in range(1, NY):
@@ -186,9 +186,39 @@
         )
         copy.start()
         copies.append(copy)
+
+    own_order = jnp.where(iota((8, 128), 1) == 2 * sim, m_row, 0)
+    first = jnp.sum((own_order >> 7).astype(F32), axis=1, keepdims=True)[0:1]
+    first16 = jnp.broadcast_to(first, (16, 128))
+    below = [jnp.clip(first16 - p, 0.0, 1.0) for p in range(-1, 64)]
+    for copy, panel, compact in ((l_copy, lv, lc), (s_copy, sv, sc)):
+        copy.wait()
+        for r in range(0, 64, 16):
+            last = jnp.zeros((16, BLOCK), BF16)
+            for p in range(64):
+                up, at = divmod(p, HALF)
+                one = panel[0, r : r + 16, BLOCK * p : BLOCK * p + BLOCK]
+                two = panel[1, r : r + 16, BLOCK * (63 - p) : BLOCK * (64 - p)]
+                mixed = one * (1.0 - below[p + 1]).astype(BF16) + two * below[p + 1].astype(BF16)
+                last = last + two * (below[p] - below[p + 1]).astype(BF16)
+                compact[64 * up + r : 64 * up + r + 16, BLOCK * at : BLOCK * at + BLOCK] = mixed
+            compact[64 + r : 64 + r + 16, WIDE - 2 * BLOCK : WIDE - BLOCK] = last
+            compact[64 + r : 64 + r + 16, WIDE - BLOCK : WIDE] = jnp.zeros((16, BLOCK), BF16)
+    first = jnp.broadcast_to(first, (4, WIDE)).astype(jnp.int32)
+    position = (iota((4, WIDE), 1) >> 7) + HALF * (iota((4, WIDE), 0) >> 1)
+    second = (position < first) | (position >= 64)
+    block = jnp.where(position < first, 63 - position, jnp.where(position >= 64, 63 - first, position))
+    ell = (BLOCK * block + (iota((4, WIDE), 1) & 127)).astype(F32)
+    factor[...] = jnp.where(
+        ell >= 2.0,
+        jnp.sqrt((ell + 2.0) * (ell - 1.0) / jnp.maximum(ell * (ell + 1.0), 1.0)),
+        0.0,
+    )
+
     for copy in copies:
         copy.wait_recv()
     summed[...] = part[pl.ds(y * NZ, NZ)] + recv_y[0] + (recv_y[1] + recv_y[2])
+    pl.semaphore_wait(far, 2)
     for d in range(1, NZ):
         z_to = (z + d) % NZ
         copy = pltpu.make_async_remote_copy(
@@ -201,8 +231,6 @@
         )
         copy.start()
         copies.append(copy)
-    l_copy.wait()
-    s_copy.wait()
     for copy in copies[NY - 1 :]:
         copy.wait_recv()
     modes = summed[z]
@@ -210,80 +238,69 @@
         modes = modes + recv_z[d]
 
     side = iota((2, 128), 1) < 64
-    rows4 = jnp.concatenate(
+    other = pltpu.roll(modes, 64, 1)
+    rows8 = jnp.concatenate(
         [
             jnp.where(side, modes, 0.0),
+            jnp.where(side, 0.0, other),
+            jnp.where(side, other, 0.0),
             jnp.where(side, 0.0, modes),
-            jnp.zeros((4, 128), F32),
         ],
         axis=0,
     ).astype(BF16)
-    for i in range(NLENS):
-        columns = slice(LCHUNK * i, LCHUNK * (i + 1))
-        kappa = mxu(rows4, lv[:, :, columns].reshape(128, LCHUNK))
-        kpart[i] = kappa[0:4].astype(BF16)
-
     copies_k = []
-    for d in range(1, NLENS):
-        lens_to = (lens + d) % NLENS
-        copy = pltpu.make_async_remote_copy(
-            src_ref=kpart.at[lens_to],
-            dst_ref=recv_k.at[d - 1],
-            send_sem=send_k.at[d - 1],
-            recv_sem=got_k.at[d - 1],
-            device_id=(sim, lens_to),
-            device_id_type=MESH,
-        )
-        copy.start()
-        copies_k.append(copy)
-    for copy in copies_k:
-        copy.wait_recv()
-    kappa = kpart[lens].astype(F32)
-    for d in range(NLENS - 1):
-        kappa = kappa + recv_k[d].astype(F32)
-    kfull[lens] = kappa.astype(BF16)
-    copies_g = []
-    for d in range(1, NLENS):
-        lens_to = (lens + d) % NLENS
-        copy = pltpu.make_async_remote_copy(
-            src_ref=kfull.at[lens],
-            dst_ref=kfull.at[lens],
-            send_sem=send_g.at[d - 1],
-            recv_sem=got_g.at[d - 1],
-            device_id=(sim, lens_to),
-            device_id_type=MESH,
-        )
-        copy.start()
-        copies_g.append(copy)
-    for copy in copies_g:
-        copy.wait_recv()
-
-    pad = jnp.zeros((4, LCHUNK), F32)
+    for i, (start, end) in enumerate(CHUNKS):
+        lanes = slice(BLOCK * start, BLOCK * end)
+        kappa = mxu(rows8, lc[:, lanes])
+        kpart[:, lanes] = jnp.where(second[:, lanes], kappa[4:8], kappa[0:4]).astype(BF16)
+        window = pl.ds(BLOCK * start, BLOCK * (end - start))
+        for d in range(1, NLENS):
+            lens_to = (lens + d) % NLENS
+            copy = pltpu.make_async_remote_copy(
+                src_ref=kpart.at[:, window],
+                dst_ref=recv_k.at[d - 1, :, window],
+                send_sem=send_k.at[d - 1, i],
+                recv_sem=got_k.at[d - 1, i],
+                device_id=(sim, lens_to),
+                device_id_type=MESH,
+            )
+            copy.start()
+            copies_k.append(copy)
+
     out_k = jnp.zeros((8, 128), F32)
     out_s = jnp.zeros((8, 128), F32)
     contract = (((1,), (1,)), ((), ()))
-    for i in range(NLENS):
-        columns = slice(LCHUNK * i, LCHUNK * (i + 1))
-        kappa = jnp.concatenate([kfull[i].astype(F32), pad], axis=0)
-        shear = kappa * factor[i : i + 1, :]
-        out_k = out_k + lax.dot_general(
-            kappa.astype(BF16),
-            lv[:, :, columns].reshape(128, LCHUNK),
-            contract,
-            preferred_element_type=F32,
-        )
-        out_s = out_s + lax.dot_general(
-            shear.astype(BF16),
-            sv[:, :, columns].reshape(128, LCHUNK),
-            contract,
-            preferred_element_type=F32,
-        )
+    for i, (start, end) in enumerate(CHUNKS):
+        lanes = slice(BLOCK * start, BLOCK * end)
+        kappa = kpart[:, lanes].astype(F32)
+        for d in range(NLENS - 1):
+            copies_k[(NLENS - 1) * i + d].wait_recv()
+            kappa = kappa + recv_k[d, :, lanes].astype(F32)
+        zero = jnp.zeros_like(kappa)
+        of_second = second[:, lanes]
+        shear = kappa * factor[:, lanes]
+        for value, panel, kind in ((kappa, lc, 0), (shear, sc, 1)):
+            value8 = jnp.concatenate(
+                [jnp.where(of_second, zero, value), jnp.where(of_second, value, zero)], axis=0
+            )
+            out = lax.dot_general(
+                value8.astype(BF16), panel[:, lanes], contract, preferred_element_type=F32
+            )
+            if kind == 0:
+                out_k = out_k + out
+            else:
+                out_s = out_s + out
     scale = 1.0 / math.sqrt(LMAX)
-    for b in range(2):
-        kappa_out[b] = out_k[2 * b : 2 * b + 2, 64 * b : 64 * b + 64] * scale
-        shear_out[b] = out_s[2 * b : 2 * b + 2, 64 * b : 64 * b + 64] * scale
-    for copy in copies + copies_k + copies_g:
+    raw[0] = out_k * scale
+    raw[1] = out_s * scale
+    for copy in copies + copies_k:
         copy.wait_send()
+
+
+def finish(raw, kappa_out, shear_out):
+    for kind, out in ((0, kappa_out), (1, shear_out)):
+        for b in range(2):
+            out[b] = raw[kind, 4 * b : 4 * b + 2, 0:64] + raw[kind, 4 * b + 2 : 4 * b + 4, 64:128]
 
 
 def on_device(
@@ -291,41 +308,42 @@
 ):
     hbm = pl.BlockSpec(memory_space=pl.ANY)
     vmem = pl.BlockSpec(memory_space=pltpu.VMEM)
+    smem = pl.BlockSpec(memory_space=pltpu.SMEM)
     shape = jax.ShapeDtypeStruct((2, 2, 64), F32)
     dma = pltpu.SemaphoreType.DMA
-    return pl.pallas_call(
+    raw = pl.pallas_call(
         kernel,
-        out_shape=(shape, shape),
-        in_specs=[hbm, hbm, hbm, pl.BlockSpec(memory_space=pltpu.SMEM), hbm, hbm, hbm],
-        out_specs=(vmem, vmem),
+        out_shape=jax.ShapeDtypeStruct((2, 8, 128), F32),
+        in_specs=[hbm, hbm, hbm, smem, hbm, hbm, hbm],
+        out_specs=vmem,
         scratch_shapes=[
             pltpu.VMEM((3, 1, 128), jnp.int32),
             pltpu.VMEM((K_DEV, SHELLS, BPX), BF16),
             pltpu.VMEM((2, 64, LMAX), BF16),
             pltpu.VMEM((2, 64, LMAX), BF16),
+            pltpu.VMEM((128, WIDE), BF16),
+            pltpu.VMEM((128, WIDE), BF16),
             pltpu.VMEM((BPX, 256), BF16),
             pltpu.VMEM((BPX, 256), BF16),
             pltpu.VMEM((2, 32, 128), F32),
             pltpu.VMEM((2, ROWS, 128), F32),
-            pltpu.VMEM((8, LCHUNK), F32),
+            pltpu.VMEM((4, WIDE), F32),
             pltpu.VMEM((NY * NZ, 2, 128), F32),
             pltpu.VMEM((NY - 1, NZ, 2, 128), F32),
             pltpu.VMEM((NZ, 2, 128), F32),
             pltpu.VMEM((NZ - 1, 2, 128), F32),
-            pltpu.VMEM((NLENS, 4, LCHUNK), BF16),
-            pltpu.VMEM((NLENS - 1, 4, LCHUNK), BF16),
-            pltpu.VMEM((NLENS, 4, LCHUNK), BF16),
+            pltpu.VMEM((4, WIDE), BF16),
+            pltpu.VMEM((NLENS - 1, 4, WIDE), BF16),
             dma((3,)),
             dma((4,)),
             dma((2,)),
+            pltpu.SemaphoreType.REGULAR,
             dma((NY - 1,)),
             dma((NY - 1,)),
             dma((NZ - 1,)),
             dma((NZ - 1,)),
-            dma((NLENS - 1,)),
-            dma((NLENS - 1,)),
-            dma((NLENS - 1,)),
-            dma((NLENS - 1,)),
+            dma((NLENS - 1, len(CHUNKS))),
+            dma((NLENS - 1, len(CHUNKS))),
         ],
         compiler_params=pltpu.CompilerParams(collective_id=0, has_side_effects=True),
         name="shear_step",
@@ -338,6 +356,13 @@
         legendre_panel,
         spin2_panel,
     )
+    return pl.pallas_call(
+        finish,
+        out_shape=(shape, shape),
+        in_specs=[vmem],
+        out_specs=(vmem, vmem),
+        name="finish",
+    )(raw)
 
 
 def solution(mesh):

time: 42.3 us -> 37.5 us (0.89)
  local copies, waits for them, and re-layouts: 2.48 us -> 0 us
  Pallas kernels: 39 us -> 36.7 us
    unnamed x2 -> x0, local copies, waits for them, and re-layouts: 2.48 us -> none
    pallas_call x1 -> x2, Pallas kernels: 39 us -> 36.7 us  [the longest x1 35.3 us: on_device(): pl.pallas_call(kernel, out_shape=jax.ShapeDtypeStruct((2, 8, 128), F32),...]
where the time goes in v2:
time: 37.5 us; the launch traced here: 37.3 us
  Pallas kernels  36.7 us (98%)
  between operations  0.64 us (2%)
    pallas_call x1, Pallas kernels, on_device(): pl.pallas_call(kernel, out_shape=jax.ShapeDtypeStruct((2, 8, 128), F32),...  35.3 us
    pallas_call x1, Pallas kernels, on_device(): pl.pallas_call(finish, out_shape=(shape, shape), in_specs=[vmem], out_spe...  1.35 us

profile of v2, /device:TPU:1, one launch (start us, length us, event | category | flops | bytes accessed | tf_op | source)
XLA Modules:
  0.0 37.3 jit_solution(407967884614311790)
XLA Ops:
  0.6 35.3 %shear_step.1.raw = f32[2,8,128]{2,1,0:T(8,128)} custom-call(s32[1,128]{1,0:T(1,128)} %bitcast.3, s32[1,128]{1,0:T(1,128)} %bitcast.4, s32[1,128]{1,0:T(1,128)} %bitcast.5, f32[2]{0:T(128)} %weight.1, bf16[128,2,2048]{2,1,0:T(2,128)(2,1)} %x_hbm.1, bf16[2,64,8192]{2,1,0:T(8,128)(2,1)} %l_hbm.1, bf16[2,64,8192]{2,1,0:T(8,128)(2,1)} %s_hbm.1), custom_call_target="tpu_custom_call" | custom-call | tf_op jit(solution)/shard_map/shear_step/pallas_call | solution.py:314
  36.0 1.4 %finish.1 = (f32[2,2,64]{2,1,0:T(2,128)}, f32[2,2,64]{2,1,0:T(2,128)}) custom-call(f32[2,8,128]{2,1,0:T(8,128)} %shear_step.1.raw), custom_call_target="tpu_custom_call" | custom-call | tf_op jit(solution)/shard_map/finish/pallas_call | solution.py:359

commit v3 on v2

--- a/solution.py
+++ b/solution.py
@@ -20,7 +20,9 @@
 HALF = 33
 WIDE = HALF * BLOCK
 CHUNKS = ((0, 12), (12, 24), (24, 33))
-NEAR = 4
+NH = NZ // 2
+HUB = NH // 2
+FAR_FIRST = (0, 1, 7, 2, 6, 3, 5, 4)
 MESH = pl.DeviceIdType.MESH
 F32 = jnp.float32
 BF16 = jnp.bfloat16
@@ -54,12 +56,12 @@
 
 
 def kernel(
-    cycle_hbm, block_hbm, m_hbm, weight, x_hbm, l_hbm, s_hbm,
+    cycle_hbm, block_hbm, m_hbm, weight_hbm, x_hbm, l_hbm, s_hbm,
     raw,
-    small, xv, lv, sv, lc, sc, table_hi, table_lo, base, turn, factor,
-    part, recv_y, summed, recv_z, kpart, recv_k,
-    small_sem, x_sem, panel_sem, far,
-    send_y, got_y, send_z, got_z, send_k, got_k,
+    small, weight, xv, lv, sv, lc, sc, table_hi, table_lo, base, turn, factor,
+    part, recv_y, summed, recv_z, recv_x, kpart, recv_k,
+    small_sem, x_sem, panel_sem, far, met,
+    send_y, got_y, send_z, got_z, send_x, got_x, send_k, got_k,
 ):
     sim = lax.axis_index("sim")
     lens = lax.axis_index("lens")
@@ -70,11 +72,10 @@
         return (z_to * NY + y_to, lens)
 
     barrier = pltpu.get_barrier_semaphore()
-    near = [d for d in range(1, NZ) if min(d, NZ - d) <= NEAR]
-    for d in near:
-        pl.semaphore_signal(
-            barrier, inc=1, device_id=sim_id((z + d) % NZ, y), device_id_type=MESH
-        )
+    half = z // NH
+    across = (1 - half) * NH
+    own = half * NH
+    place = z % NH
     for d in range(1, NY):
         pl.semaphore_signal(
             barrier, inc=1, device_id=sim_id(z, (y + d) % NY), device_id_type=MESH
@@ -83,11 +84,28 @@
         pl.semaphore_signal(
             barrier, inc=1, device_id=(sim, (lens + d) % NLENS), device_id_type=MESH
         )
+
+    @pl.when(place != HUB)
+    def _():
+        pl.semaphore_signal(barrier, inc=1, device_id=sim_id(own + HUB, y), device_id_type=MESH)
+
+    @pl.when(half == 0)
+    def _():
+        for e in range(NH):
+            for dy in range(NY):
+                pl.semaphore_signal(
+                    barrier,
+                    inc=1,
+                    device_id=sim_id(NH + (place + e) % NH, (y + dy) % NY),
+                    device_id_type=MESH,
+                )
+
 
     small_copies = [
         pltpu.make_async_copy(source, small.at[i], small_sem.at[i])
         for i, source in enumerate((cycle_hbm, block_hbm, m_hbm))
     ]
+    small_copies.append(pltpu.make_async_copy(weight_hbm, weight, small_sem.at[3]))
     for copy in small_copies:
         copy.start()
     x_copies = [
@@ -140,7 +158,7 @@
     phase = (code_column >> 6) * (2 * BPX) + (code_column & 1)
     turn_cos, turn_sin = cos_sin((phase * orders) & 32767)
     scale = 1.0 / (math.sqrt(NPIX) * math.sqrt(NZ * NY * NLENS))
-    row_weight = jnp.where((row2 & 1) == 0, weight[0], weight[1]) * scale
+    row_weight = jnp.where((row2 & 1) == 0, weight[0:1, 0:1], weight[0:1, 1:2]) * scale
     turn[0] = turn_cos * row_weight
     turn[1] = turn_sin * row_weight
     spread = (iota((128, ROWS), 0) == (iota((128, ROWS), 1) >> 1)).astype(BF16)
@@ -169,15 +187,48 @@
         turned = gathered[:, 128 * c : 128 * c + 128].T
         part[:, c, :] = jnp.where(left, turned[0:64], turned[64:128])
 
-    pl.semaphore_wait(barrier, len(near) + NY - 1 + NLENS - 1)
-    for d in (NEAR, NZ - NEAR):
-        pl.semaphore_signal(far, inc=1, device_id=sim_id((z + d) % NZ, y), device_id_type=MESH)
+    is_hub = (place == HUB).astype(jnp.int32)
+    pl.semaphore_wait(barrier, NY - 1 + NLENS - 1 + half * (NH * NY) + is_hub * (NH - 1))
+
+    @pl.when(half == 1)
+    def _():
+        for e in range(NH):
+            pl.semaphore_signal(
+                met, inc=1, device_id=sim_id((place + e) % NH, y), device_id_type=MESH
+            )
+
+    @pl.when(place == HUB)
+    def _():
+        for d in range(1, NH):
+            pl.semaphore_signal(
+                far, inc=1, device_id=sim_id(own + (place + d) % NH, y), device_id_type=MESH
+            )
+
+    copies_x = []
+    for e in FAR_FIRST:
+        for dy in (2, 1, 3, 0):
+            z_to, y_to = across + (place + e) % NH, (y + dy) % NY
+            copies_x.append(
+                pltpu.make_async_remote_copy(
+                    src_ref=part.at[y_to * NZ + z_to],
+                    dst_ref=recv_x.at[e * NY + dy],
+                    send_sem=send_x.at[e * NY + dy],
+                    recv_sem=got_x.at[e * NY + dy],
+                    device_id=sim_id(z_to, y_to),
+                    device_id_type=MESH,
+                )
+            )
+
+    @pl.when(half == 1)
+    def _():
+        for copy in copies_x:
+            copy.start()
 
     copies = []
     for d in range(1, NY):
         y_to = (y + d) % NY
         copy = pltpu.make_async_remote_copy(
-            src_ref=part.at[pl.ds(y_to * NZ, NZ)],
+            src_ref=part.at[pl.ds(y_to * NZ + own, NH)],
             dst_ref=recv_y.at[d - 1],
             send_sem=send_y.at[d - 1],
             recv_sem=got_y.at[d - 1],
@@ -217,25 +268,39 @@
 
     for copy in copies:
         copy.wait_recv()
-    summed[...] = part[pl.ds(y * NZ, NZ)] + recv_y[0] + (recv_y[1] + recv_y[2])
-    pl.semaphore_wait(far, 2)
-    for d in range(1, NZ):
-        z_to = (z + d) % NZ
+    summed[...] = part[pl.ds(y * NZ + own, NH)] + recv_y[0] + (recv_y[1] + recv_y[2])
+    @pl.when(place != HUB)
+    def _():
+        pl.semaphore_wait(far, 1)
+
+    for d in range(1, NH):
+        i_to = (place + d) % NH
         copy = pltpu.make_async_remote_copy(
-            src_ref=summed.at[z_to],
+            src_ref=summed.at[i_to],
             dst_ref=recv_z.at[d - 1],
             send_sem=send_z.at[d - 1],
             recv_sem=got_z.at[d - 1],
-            device_id=sim_id(z_to, y),
+            device_id=sim_id(own + i_to, y),
             device_id_type=MESH,
         )
         copy.start()
         copies.append(copy)
+
+    @pl.when(half == 0)
+    def _():
+        pl.semaphore_wait(met, NH)
+        for copy in copies_x:
+            copy.start()
+
     for copy in copies[NY - 1 :]:
         copy.wait_recv()
-    modes = summed[z]
-    for d in range(NZ - 1):
+    modes = summed[place]
+    for d in range(NH - 1):
         modes = modes + recv_z[d]
+    for copy in copies_x:
+        copy.wait_recv()
+    for n in range(NH * NY):
+        modes = modes + recv_x[n]
 
     side = iota((2, 128), 1) < 64
     other = pltpu.roll(modes, 64, 1)
@@ -293,7 +358,7 @@
     scale = 1.0 / math.sqrt(LMAX)
     raw[0] = out_k * scale
     raw[1] = out_s * scale
-    for copy in copies + copies_k:
+    for copy in copies + copies_x + copies_k:
         copy.wait_send()
 
 
@@ -306,18 +371,30 @@
 def on_device(
     patches, patch_cycle, patch_block, m_values, shell_weight, legendre_panel, spin2_panel
 ):
-    hbm = pl.BlockSpec(memory_space=pl.ANY)
+    hbm = pl.BlockSpec(memory_space=pltpu.HBM)
     vmem = pl.BlockSpec(memory_space=pltpu.VMEM)
-    smem = pl.BlockSpec(memory_space=pltpu.SMEM)
     shape = jax.ShapeDtypeStruct((2, 2, 64), F32)
     dma = pltpu.SemaphoreType.DMA
+    operands = [
+        pltpu.with_memory_space_constraint(operand, pltpu.HBM)
+        for operand in (
+            patch_cycle.reshape(1, K_DEV),
+            patch_block.reshape(1, K_DEV),
+            m_values.reshape(1, 128),
+            shell_weight.reshape(1, SHELLS),
+            patches,
+            legendre_panel,
+            spin2_panel,
+        )
+    ]
     raw = pl.pallas_call(
         kernel,
         out_shape=jax.ShapeDtypeStruct((2, 8, 128), F32),
-        in_specs=[hbm, hbm, hbm, smem, hbm, hbm, hbm],
+        in_specs=[hbm] * 7,
         out_specs=vmem,
         scratch_shapes=[
             pltpu.VMEM((3, 1, 128), jnp.int32),
+            pltpu.VMEM((1, SHELLS), F32),
             pltpu.VMEM((K_DEV, SHELLS, BPX), BF16),
             pltpu.VMEM((2, 64, LMAX), BF16),
             pltpu.VMEM((2, 64, LMAX), BF16),
@@ -329,38 +406,35 @@
             pltpu.VMEM((2, ROWS, 128), F32),
             pltpu.VMEM((4, WIDE), F32),
             pltpu.VMEM((NY * NZ, 2, 128), F32),
-            pltpu.VMEM((NY - 1, NZ, 2, 128), F32),
-            pltpu.VMEM((NZ, 2, 128), F32),
-            pltpu.VMEM((NZ - 1, 2, 128), F32),
+            pltpu.VMEM((NY - 1, NH, 2, 128), F32),
+            pltpu.VMEM((NH, 2, 128), F32),
+            pltpu.VMEM((NH - 1, 2, 128), F32),
+            pltpu.VMEM((NH * NY, 2, 128), F32),
             pltpu.VMEM((4, WIDE), BF16),
             pltpu.VMEM((NLENS - 1, 4, WIDE), BF16),
-            dma((3,)),
+            dma((4,)),
             dma((4,)),
             dma((2,)),
             pltpu.SemaphoreType.REGULAR,
+            pltpu.SemaphoreType.REGULAR,
             dma((NY - 1,)),
             dma((NY - 1,)),
-            dma((NZ - 1,)),
-            dma((NZ - 1,)),
+            dma((NH - 1,)),
+            dma((NH - 1,)),
+            dma((NH * NY,)),
+            dma((NH * NY,)),
             dma((NLENS - 1, len(CHUNKS))),
             dma((NLENS - 1, len(CHUNKS))),
         ],
-        compiler_params=pltpu.CompilerParams(collective_id=0, has_side_effects=True),
+        compiler_params=pltpu.CompilerParams(collective_id=0, has_side_effects=True, vmem_limit_bytes=24 << 20),
         name="shear_step",
-    )(
-        patch_cycle.reshape(1, K_DEV),
-        patch_block.reshape(1, K_DEV),
-        m_values.reshape(1, 128),
-        shell_weight,
-        patches,
-        legendre_panel,
-        spin2_panel,
-    )
+    )(*operands)
     return pl.pallas_call(
         finish,
         out_shape=(shape, shape),
         in_specs=[vmem],
         out_specs=(vmem, vmem),
+        compiler_params=pltpu.CompilerParams(vmem_limit_bytes=1 << 20),
         name="finish",
     )(raw)
 

time: 37.5 us -> 33.6 us (0.90)
  Pallas kernels: 36.7 us -> 32.8 us
    pallas_call x1, Pallas kernels: 35.3 us -> 32.2 us  [on_device(): pl.pallas_call(kernel, out_shape=jax.ShapeDtypeStruct((2, 8, 128), F32),...]
    pallas_call x1, Pallas kernels: 1.35 us -> 0.65 us  [on_device(): pl.pallas_call(finish, out_shape=(shape, shape), in_specs=[vmem], out_spe...]
where the time goes in v3:
time: 33.6 us; the launch traced here: 33.5 us
  Pallas kernels  32.8 us (98%)
  between operations  0.64 us (2%)
    pallas_call x1, Pallas kernels, on_device(): pl.pallas_call(kernel, out_shape=jax.ShapeDtypeStruct((2, 8, 128), F32),...  32.2 us

profile of v3, /device:TPU:1, one launch (start us, length us, event | category | flops | bytes accessed | tf_op | source)
XLA Modules:
  0.0 33.5 jit_solution(8192878282329390631)
XLA Ops:
  0.6 32.2 %shear_step.1.raw = f32[2,8,128]{2,1,0:T(8,128)S(1)} custom-call(s32[1,128]{1,0:T(1,128)} %bitcast.4, s32[1,128]{1,0:T(1,128)} %bitcast.5, s32[1,128]{1,0:T(1,128)} %bitcast.6, f32[1,2]{1,0:T(1,128)} %bitcast.7, bf16[128,2,2048]{2,1,0:T(2,128)(2,1)} %x_hbm.1, bf16[2,64,8192]{2,1,0:T(8,128)(2,1)} %l_hbm.1, bf16[2,64,8192]{2,1,0:T(8,128)(2,1)} %s_hbm.1), custom_call_target="tpu_custom_call" | custom-call | tf_op jit(solution)/shard_map/shear_step/pallas_call | solution.py:390
  32.8 0.7 %finish.1 = (f32[2,2,64]{2,1,0:T(2,128)}, f32[2,2,64]{2,1,0:T(2,128)}) custom-call(f32[2,8,128]{2,1,0:T(8,128)S(1)} %shear_step.1.raw), custom_call_target="tpu_custom_call" | custom-call | tf_op jit(solution)/shard_map/finish/pallas_call | solution.py:432

commit v4 on v3

--- a/solution.py
+++ b/solution.py
@@ -28,11 +28,6 @@
 BF16 = jnp.bfloat16
 
 
-def split(value):
-    high = value.astype(BF16)
-    return high, (value - high.astype(F32)).astype(BF16)
-
-
 def mxu(a, b):
     return jnp.dot(a, b, preferred_element_type=F32)
 
@@ -58,8 +53,8 @@
 def kernel(
     cycle_hbm, block_hbm, m_hbm, weight_hbm, x_hbm, l_hbm, s_hbm,
     raw,
-    small, weight, xv, lv, sv, lc, sc, table_hi, table_lo, base, turn, factor,
-    part, recv_y, summed, recv_z, recv_x, kpart, recv_k,
+    small, weight, xv, lv, sv, lc, sc, table, base, turn, factor,
+    staged, part, recv_y, summed, recv_z, recv_x, kpart, recv_k,
     small_sem, x_sem, panel_sem, far, met,
     send_y, got_y, send_z, got_z, send_x, got_x, send_k, got_k,
 ):
@@ -70,36 +65,6 @@
 
     def sim_id(z_to, y_to):
         return (z_to * NY + y_to, lens)
-
-    barrier = pltpu.get_barrier_semaphore()
-    half = z // NH
-    across = (1 - half) * NH
-    own = half * NH
-    place = z % NH
-    for d in range(1, NY):
-        pl.semaphore_signal(
-            barrier, inc=1, device_id=sim_id(z, (y + d) % NY), device_id_type=MESH
-        )
-    for d in range(1, NLENS):
-        pl.semaphore_signal(
-            barrier, inc=1, device_id=(sim, (lens + d) % NLENS), device_id_type=MESH
-        )
-
-    @pl.when(place != HUB)
-    def _():
-        pl.semaphore_signal(barrier, inc=1, device_id=sim_id(own + HUB, y), device_id_type=MESH)
-
-    @pl.when(half == 0)
-    def _():
-        for e in range(NH):
-            for dy in range(NY):
-                pl.semaphore_signal(
-                    barrier,
-                    inc=1,
-                    device_id=sim_id(NH + (place + e) % NH, (y + dy) % NY),
-                    device_id_type=MESH,
-                )
-
 
     small_copies = [
         pltpu.make_async_copy(source, small.at[i], small_sem.at[i])
@@ -116,6 +81,36 @@
     ]
     for copy in x_copies:
         copy.start()
+    barrier = pltpu.get_barrier_semaphore()
+    half = z // NH
+    across = (1 - half) * NH
+    own = half * NH
+    place = z % NH
+    for d in range(1, NY):
+        pl.semaphore_signal(
+            barrier, inc=1, device_id=sim_id(z, (y + d) % NY), device_id_type=MESH
+        )
+    for d in range(1, NLENS):
+        pl.semaphore_signal(
+            barrier, inc=1, device_id=(sim, (lens + d) % NLENS), device_id_type=MESH
+        )
+
+    @pl.when(place != HUB)
+    def _():
+        pl.semaphore_signal(barrier, inc=1, device_id=sim_id(own + HUB, y), device_id_type=MESH)
+
+    @pl.when(half == 0)
+    def _():
+        for e in range(NH):
+            for dy in range(NY):
+                pl.semaphore_signal(
+                    barrier,
+                    inc=1,
+                    device_id=sim_id(NH + (place + e) % NH, (y + dy) % NY),
+                    device_id_type=MESH,
+                )
+
+
     l_copy = pltpu.make_async_copy(l_hbm, lv, panel_sem.at[0])
     s_copy = pltpu.make_async_copy(s_hbm, sv, panel_sem.at[1])
     for copy in small_copies:
@@ -141,12 +136,8 @@
         ca = base[0, pl.ds(a, 1), :]
         sa = base[1, pl.ds(a, 1), :]
         rows = pl.ds(pl.multiple_of(a * 64, 64), 64)
-        c_high, c_low = split(ca * b_cos - sa * b_sin)
-        s_high, s_low = split(sa * b_cos + ca * b_sin)
-        table_hi[rows, 0:128] = c_high
-        table_hi[rows, 128:256] = s_high
-        table_lo[rows, 0:128] = c_low
-        table_lo[rows, 128:256] = s_low
+        table[rows, 0:128] = (ca * b_cos - sa * b_sin).astype(BF16)
+        table[rows, 128:256] = (sa * b_cos + ca * b_sin).astype(BF16)
         return carry
 
     lax.fori_loop(0, 32, fill, 0)
@@ -167,25 +158,21 @@
     )[0:1]
     onehot = ((iota((128, ROWS), 0) & 63).astype(F32) == cycle_wide).astype(F32).astype(BF16)
 
-    total = jnp.zeros((ROWS, 256), F32)
-    for i in range(8):
-        if i % 2 == 0:
-            x_copies[i // 2].wait()
-        piece = xv[:, :, 256 * i : 256 * i + 256].reshape(ROWS, 256)
-        total = total + mxu(piece, table_hi[256 * i : 256 * i + 256])
-        total = total + mxu(piece, table_lo[256 * i : 256 * i + 256])
+    for copy in x_copies:
+        copy.wait()
+    total = mxu(xv[...].reshape(ROWS, BPX), table[...])
     l_copy.start()
     s_copy.start()
     zc = total[:, 0:128]
     zs = total[:, 128:256]
     real = turn[0] * zc - turn[1] * zs
     imag = -(turn[1] * zc + turn[0] * zs)
-    high, low = split(jnp.concatenate([real, imag], axis=1))
-    gathered = mxu(onehot, high) + mxu(onehot, low)
+    gathered = mxu(onehot, jnp.concatenate([real, imag], axis=1).astype(BF16))
     left = iota((64, 128), 1) < 64
     for c in range(2):
         turned = gathered[:, 128 * c : 128 * c + 128].T
-        part[:, c, :] = jnp.where(left, turned[0:64], turned[64:128])
+        staged[:, c, :] = jnp.where(left, turned[0:64], turned[64:128])
+    part[...] = staged[...].astype(BF16)
 
     is_hub = (place == HUB).astype(jnp.int32)
     pl.semaphore_wait(barrier, NY - 1 + NLENS - 1 + half * (NH * NY) + is_hub * (NH - 1))
@@ -268,7 +255,8 @@
 
     for copy in copies:
         copy.wait_recv()
-    summed[...] = part[pl.ds(y * NZ + own, NH)] + recv_y[0] + (recv_y[1] + recv_y[2])
+    here = part[pl.ds(y * NZ + own, NH)].astype(F32) + recv_y[0].astype(F32)
+    summed[...] = here + (recv_y[1].astype(F32) + recv_y[2].astype(F32))
     @pl.when(place != HUB)
     def _():
         pl.semaphore_wait(far, 1)
@@ -300,7 +288,7 @@
     for copy in copies_x:
         copy.wait_recv()
     for n in range(NH * NY):
-        modes = modes + recv_x[n]
+        modes = modes + recv_x[n].astype(F32)
 
     side = iota((2, 128), 1) < 64
     other = pltpu.roll(modes, 64, 1)
@@ -401,15 +389,15 @@
             pltpu.VMEM((128, WIDE), BF16),
             pltpu.VMEM((128, WIDE), BF16),
             pltpu.VMEM((BPX, 256), BF16),
-            pltpu.VMEM((BPX, 256), BF16),
             pltpu.VMEM((2, 32, 128), F32),
             pltpu.VMEM((2, ROWS, 128), F32),
             pltpu.VMEM((4, WIDE), F32),
             pltpu.VMEM((NY * NZ, 2, 128), F32),
-            pltpu.VMEM((NY - 1, NH, 2, 128), F32),
+            pltpu.VMEM((NY * NZ, 2, 128), BF16),
+            pltpu.VMEM((NY - 1, NH, 2, 128), BF16),
             pltpu.VMEM((NH, 2, 128), F32),
             pltpu.VMEM((NH - 1, 2, 128), F32),
-            pltpu.VMEM((NH * NY, 2, 128), F32),
+            pltpu.VMEM((NH * NY, 2, 128), BF16),
             pltpu.VMEM((4, WIDE), BF16),
             pltpu.VMEM((NLENS - 1, 4, WIDE), BF16),
             dma((4,)),

time: 33.6 us -> 32.1 us (0.955)
  Pallas kernels: 32.8 us -> 31.3 us
    pallas_call x1, Pallas kernels: 32.2 us -> 30.7 us  [on_device(): pl.pallas_call(kernel, out_shape=jax.ShapeDtypeStruct((2, 8, 128), F32),...]
where the time goes in v4:
time: 32.1 us; the launch traced here: 32 us
  Pallas kernels  31.3 us (98%)
  between operations  0.64 us (2%)
    pallas_call x1, Pallas kernels, on_device(): pl.pallas_call(kernel, out_shape=jax.ShapeDtypeStruct((2, 8, 128), F32),...  30.7 us
    pallas_call x1, Pallas kernels, on_device(): pl.pallas_call(finish, out_shape=(shape, shape), in_specs=[vmem], out_spe...  0.65 us

profile of v4, /device:TPU:1, one launch (start us, length us, event | category | flops | bytes accessed | tf_op | source)
XLA Modules:
  0.0 32.0 jit_solution(3407860114766274859)
XLA Ops:
  0.6 30.7 %shear_step.1.raw = f32[2,8,128]{2,1,0:T(8,128)S(1)} custom-call(s32[1,128]{1,0:T(1,128)} %bitcast.4, s32[1,128]{1,0:T(1,128)} %bitcast.5, s32[1,128]{1,0:T(1,128)} %bitcast.6, f32[1,2]{1,0:T(1,128)} %bitcast.7, bf16[128,2,2048]{2,1,0:T(2,128)(2,1)} %x_hbm.1, bf16[2,64,8192]{2,1,0:T(8,128)(2,1)} %l_hbm.1, bf16[2,64,8192]{2,1,0:T(8,128)(2,1)} %s_hbm.1), custom_call_target="tpu_custom_call" | custom-call | tf_op jit(solution)/shard_map/shear_step/pallas_call | solution.py:378
  31.3 0.7 %finish.1 = (f32[2,2,64]{2,1,0:T(2,128)}, f32[2,2,64]{2,1,0:T(2,128)}) custom-call(f32[2,8,128]{2,1,0:T(8,128)S(1)} %shear_step.1.raw), custom_call_target="tpu_custom_call" | custom-call | tf_op jit(solution)/shard_map/finish/pallas_call | solution.py:420

commit v5 on v4

--- a/solution.py
+++ b/solution.py
@@ -20,9 +20,9 @@
 HALF = 33
 WIDE = HALF * BLOCK
 CHUNKS = ((0, 12), (12, 24), (24, 33))
+LENS_ORDER = (4, 3, 5, 2, 6, 1, 7)
 NH = NZ // 2
 HUB = NH // 2
-FAR_FIRST = (0, 1, 7, 2, 6, 3, 5, 4)
 MESH = pl.DeviceIdType.MESH
 F32 = jnp.float32
 BF16 = jnp.bfloat16
@@ -54,7 +54,7 @@
     cycle_hbm, block_hbm, m_hbm, weight_hbm, x_hbm, l_hbm, s_hbm,
     raw,
     small, weight, xv, lv, sv, lc, sc, table, base, turn, factor,
-    staged, part, recv_y, summed, recv_z, recv_x, kpart, recv_k,
+    part, recv_y, summed, recv_z, recv_x, kpart, recv_k,
     small_sem, x_sem, panel_sem, far, met,
     send_y, got_y, send_z, got_z, send_x, got_x, send_k, got_k,
 ):
@@ -75,7 +75,7 @@
         copy.start()
     x_copies = [
         pltpu.make_async_copy(
-            x_hbm.at[:, :, pl.ds(512 * i, 512)], xv.at[:, :, pl.ds(512 * i, 512)], x_sem.at[i]
+            x_hbm.at[pl.ds(32 * i, 32)], xv.at[pl.ds(32 * i, 32)], x_sem.at[i]
         )
         for i in range(4)
     ]
@@ -171,8 +171,7 @@
     left = iota((64, 128), 1) < 64
     for c in range(2):
         turned = gathered[:, 128 * c : 128 * c + 128].T
-        staged[:, c, :] = jnp.where(left, turned[0:64], turned[64:128])
-    part[...] = staged[...].astype(BF16)
+        part[:, c, :] = jnp.where(left, turned[0:64], turned[64:128])
 
     is_hub = (place == HUB).astype(jnp.int32)
     pl.semaphore_wait(barrier, NY - 1 + NLENS - 1 + half * (NH * NY) + is_hub * (NH - 1))
@@ -192,16 +191,16 @@
             )
 
     copies_x = []
-    for e in FAR_FIRST:
-        for dy in (2, 1, 3, 0):
-            z_to, y_to = across + (place + e) % NH, (y + dy) % NY
+    for n in range(NH):
+        for y_to in range(NY):
+            at = (n - place + NH) % NH * NY + (y_to - y + NY) % NY
             copies_x.append(
                 pltpu.make_async_remote_copy(
-                    src_ref=part.at[y_to * NZ + z_to],
-                    dst_ref=recv_x.at[e * NY + dy],
-                    send_sem=send_x.at[e * NY + dy],
-                    recv_sem=got_x.at[e * NY + dy],
-                    device_id=sim_id(z_to, y_to),
+                    src_ref=part.at[y_to * NZ + across + n],
+                    dst_ref=recv_x.at[at],
+                    send_sem=send_x.at[at],
+                    recv_sem=got_x.at[at],
+                    device_id=sim_id(across + n, y_to),
                     device_id_type=MESH,
                 )
             )
@@ -255,8 +254,8 @@
 
     for copy in copies:
         copy.wait_recv()
-    here = part[pl.ds(y * NZ + own, NH)].astype(F32) + recv_y[0].astype(F32)
-    summed[...] = here + (recv_y[1].astype(F32) + recv_y[2].astype(F32))
+    here = part[pl.ds(y * NZ + own, NH)] + recv_y[0]
+    summed[...] = here + (recv_y[1] + recv_y[2])
     @pl.when(place != HUB)
     def _():
         pl.semaphore_wait(far, 1)
@@ -287,8 +286,10 @@
         modes = modes + recv_z[d]
     for copy in copies_x:
         copy.wait_recv()
-    for n in range(NH * NY):
-        modes = modes + recv_x[n].astype(F32)
+    pieces = [modes] + [recv_x[n] for n in range(NH * NY)]
+    while len(pieces) > 1:
+        pieces = [sum(pieces[n : n + 2]) for n in range(0, len(pieces), 2)]
+    modes = pieces[0]
 
     side = iota((2, 128), 1) < 64
     other = pltpu.roll(modes, 64, 1)
@@ -307,7 +308,7 @@
         kappa = mxu(rows8, lc[:, lanes])
         kpart[:, lanes] = jnp.where(second[:, lanes], kappa[4:8], kappa[0:4]).astype(BF16)
         window = pl.ds(BLOCK * start, BLOCK * (end - start))
-        for d in range(1, NLENS):
+        for d in LENS_ORDER:
             lens_to = (lens + d) % NLENS
             copy = pltpu.make_async_remote_copy(
                 src_ref=kpart.at[:, window],
@@ -326,8 +327,9 @@
     for i, (start, end) in enumerate(CHUNKS):
         lanes = slice(BLOCK * start, BLOCK * end)
         kappa = kpart[:, lanes].astype(F32)
+        for copy in copies_k[(NLENS - 1) * i : (NLENS - 1) * (i + 1)]:
+            copy.wait_recv()
         for d in range(NLENS - 1):
-            copies_k[(NLENS - 1) * i + d].wait_recv()
             kappa = kappa + recv_k[d, :, lanes].astype(F32)
         zero = jnp.zeros_like(kappa)
         of_second = second[:, lanes]
@@ -393,11 +395,10 @@
             pltpu.VMEM((2, ROWS, 128), F32),
             pltpu.VMEM((4, WIDE), F32),
             pltpu.VMEM((NY * NZ, 2, 128), F32),
-            pltpu.VMEM((NY * NZ, 2, 128), BF16),
-            pltpu.VMEM((NY - 1, NH, 2, 128), BF16),
+            pltpu.VMEM((NY - 1, NH, 2, 128), F32),
             pltpu.VMEM((NH, 2, 128), F32),
             pltpu.VMEM((NH - 1, 2, 128), F32),
-            pltpu.VMEM((NH * NY, 2, 128), BF16),
+            pltpu.VMEM((NH * NY, 2, 128), F32),
             pltpu.VMEM((4, WIDE), BF16),
             pltpu.VMEM((NLENS - 1, 4, WIDE), BF16),
             dma((4,)),

time: 32.1 us -> 31.9 us (level)
  no operation moved by 1% of the time
where the time goes in v5:
time: 31.9 us; the launch traced here: 31.8 us
  Pallas kernels  31.1 us (97%)
  between operations  0.64 us (2%)
    pallas_call x1, Pallas kernels, on_device(): pl.pallas_call(kernel, out_shape=jax.ShapeDtypeStruct((2, 8, 128), F32),...  30.5 us
    pallas_call x1, Pallas kernels, on_device(): pl.pallas_call(finish, out_shape=(shape, shape), in_specs=[vmem], out_spe...  0.65 us

profile of v5, /device:TPU:1, one launch (start us, length us, event | category | flops | bytes accessed | tf_op | source)
XLA Modules:
  0.0 31.8 jit_solution(12677475397763933229)
XLA Ops:
  0.6 30.5 %shear_step.1.raw = f32[2,8,128]{2,1,0:T(8,128)S(1)} custom-call(s32[1,128]{1,0:T(1,128)} %bitcast.4, s32[1,128]{1,0:T(1,128)} %bitcast.5, s32[1,128]{1,0:T(1,128)} %bitcast.6, f32[1,2]{1,0:T(1,128)} %bitcast.7, bf16[128,2,2048]{2,1,0:T(2,128)(2,1)} %x_hbm.1, bf16[2,64,8192]{2,1,0:T(8,128)(2,1)} %l_hbm.1, bf16[2,64,8192]{2,1,0:T(8,128)(2,1)} %s_hbm.1), custom_call_target="tpu_custom_call" | custom-call | tf_op jit(solution)/shard_map/shear_step/pallas_call | solution.py:380
  31.1 0.7 %finish.1 = (f32[2,2,64]{2,1,0:T(2,128)}, f32[2,2,64]{2,1,0:T(2,128)}) custom-call(f32[2,8,128]{2,1,0:T(8,128)S(1)} %shear_step.1.raw), custom_call_target="tpu_custom_call" | custom-call | tf_op jit(solution)/shard_map/finish/pallas_call | solution.py:421

commit v6 on v5

--- a/solution.py
+++ b/solution.py
@@ -19,7 +19,7 @@
 BLOCK = 128
 HALF = 33
 WIDE = HALF * BLOCK
-CHUNKS = ((0, 12), (12, 24), (24, 33))
+CHUNKS = ((0, 14), (14, 28), (28, 33))
 LENS_ORDER = (4, 3, 5, 2, 6, 1, 7)
 NH = NZ // 2
 HUB = NH // 2
@@ -176,20 +176,6 @@
     is_hub = (place == HUB).astype(jnp.int32)
     pl.semaphore_wait(barrier, NY - 1 + NLENS - 1 + half * (NH * NY) + is_hub * (NH - 1))
 
-    @pl.when(half == 1)
-    def _():
-        for e in range(NH):
-            pl.semaphore_signal(
-                met, inc=1, device_id=sim_id((place + e) % NH, y), device_id_type=MESH
-            )
-
-    @pl.when(place == HUB)
-    def _():
-        for d in range(1, NH):
-            pl.semaphore_signal(
-                far, inc=1, device_id=sim_id(own + (place + d) % NH, y), device_id_type=MESH
-            )
-
     copies_x = []
     for n in range(NH):
         for y_to in range(NY):
@@ -209,6 +195,20 @@
     def _():
         for copy in copies_x:
             copy.start()
+
+    @pl.when(half == 1)
+    def _():
+        for e in range(NH):
+            pl.semaphore_signal(
+                met, inc=1, device_id=sim_id((place + e) % NH, y), device_id_type=MESH
+            )
+
+    @pl.when(place == HUB)
+    def _():
+        for d in range(1, NH):
+            pl.semaphore_signal(
+                far, inc=1, device_id=sim_id(own + (place + d) % NH, y), device_id_type=MESH
+            )
 
     copies = []
     for d in range(1, NY):

time: 31.9 us -> 31.9 us (level)
  no operation moved by 1% of the time
where the time goes in v6:
time: 31.9 us; the launch traced here: 31.8 us
  Pallas kernels  31.1 us (97%)
  between operations  0.64 us (2%)
    pallas_call x1, Pallas kernels, on_device(): pl.pallas_call(kernel, out_shape=jax.ShapeDtypeStruct((2, 8, 128), F32),...  30.5 us
    pallas_call x1, Pallas kernels, on_device(): pl.pallas_call(finish, out_shape=(shape, shape), in_specs=[vmem], out_spe...  0.65 us

profile of v6, /device:TPU:1, one launch (start us, length us, event | category | flops | bytes accessed | tf_op | source)
XLA Modules:
  0.0 31.8 jit_solution(4745729089966415526)
XLA Ops:
  0.6 30.5 %shear_step.1.raw = f32[2,8,128]{2,1,0:T(8,128)S(1)} custom-call(s32[1,128]{1,0:T(1,128)} %bitcast.4, s32[1,128]{1,0:T(1,128)} %bitcast.5, s32[1,128]{1,0:T(1,128)} %bitcast.6, f32[1,2]{1,0:T(1,128)} %bitcast.7, bf16[128,2,2048]{2,1,0:T(2,128)(2,1)} %x_hbm.1, bf16[2,64,8192]{2,1,0:T(8,128)(2,1)} %l_hbm.1, bf16[2,64,8192]{2,1,0:T(8,128)(2,1)} %s_hbm.1), custom_call_target="tpu_custom_call" | custom-call | tf_op jit(solution)/shard_map/shear_step/pallas_call | solution.py:380
  31.1 0.7 %finish.1 = (f32[2,2,64]{2,1,0:T(2,128)}, f32[2,2,64]{2,1,0:T(2,128)}) custom-call(f32[2,8,128]{2,1,0:T(8,128)S(1)} %shear_step.1.raw), custom_call_target="tpu_custom_call" | custom-call | tf_op jit(solution)/shard_map/finish/pallas_call | solution.py:421
